TPU v7x, 32 devices: a whole 2x2x4 slice. The times are simulated.
32 devices in a mesh: perm: 2 (over y), subj: 8 (over z, core), vert: 2 (over x).
Axes of the slice: x: 2, y: 2, z: 4, core: 2. Of those that a mesh axis runs over, the one named last changes fastest.
Arguments:
- kinship: bfloat16 [2048, 2048], P('subj')
- phenotype: bfloat16 [2048, 2048], P('subj', 'vert')
- shuffle: int32 [4096], P(('perm', 'subj')), parts along dimension 0, may hold values from 0 to 2047, as said below
Outputs:
- statistic: float32 [4096], P(('perm', 'vert')), parts along dimension 0
There are 2 independent parts, one for each index of `perm`. A program takes and returns all parts, laid end to end along the dimension named above; an argument that names none is the same for every part. Nothing has to cross between parts.
Inputs may be any that keep to these rules, and one draw needn't show every extreme that they name: shuffle is a permutation of 0 to 2047 that maps every subject into its own exchangeability block.
All inputs are finite; a program needn't handle non-finite values.
Results may differ from a plain program's by a relative error of at most 0.0003.
Values may be sent and summed in bfloat16 or wider, within the bound.
A program may use at most 128 MiB of HBM per device.

v0:
```python
import functools

import jax
import jax.numpy as jnp
from jax import lax
from jax.experimental import pallas as pl
from jax.experimental.pallas import tpu as pltpu
from jax.sharding import PartitionSpec as P

MESH = pl.DeviceIdType.MESH
CORES = 2
HALVES = 4
BEFORE = 2


def kernel(
    n_perm, n_subj,
    kin_hbm, phe_ref, shf_ref, out_ref,
    kin_ref, load_sem, waves, shuf, scol, moved_kin, gathered, acc, parts, final,
    shuf_send, shuf_recv, own_send, row_send, sib_send, row_recv, fin_send, fin_recv,
):
    perm, subj = lax.axis_index("perm"), lax.axis_index("subj")
    n_all = n_perm * n_subj
    me = perm * n_subj + subj
    z, core = subj // CORES, subj % CORES
    n_z = n_subj // CORES
    sibling = z * CORES + (1 - core)
    rows = kin_ref.shape[0]
    cols = gathered.shape[2]
    piece = rows // HALVES
    first_col = pl.multiple_of(perm * cols, cols)
    n_events = HALVES * (n_z - 1)

    def partner(k):
        other = lax.rem(me + k, n_all)
        return other, {"perm": other // n_subj, "subj": lax.rem(other, n_subj)}

    loads = (
        pltpu.make_async_copy(
            phe_ref.at[:, pl.ds(first_col, cols)], gathered.at[subj], load_sem.at[0]),
        pltpu.make_async_copy(kin_hbm, kin_ref, load_sem.at[1]),
    )
    for load in loads:
        load.start()
    barrier = pltpu.get_barrier_semaphore()

    has_left, has_right = z > 0, z < n_z - 1

    def signal(sem, **device):
        pl.semaphore_signal(sem, inc=1, device_id=device, device_id_type=MESH)

    def signal_perms(sem):
        for k in range(1, n_perm):
            signal(sem, perm=lax.rem(perm + k, n_perm))

    @pl.when(has_left)
    def _():
        signal(barrier, subj=subj - CORES)

    @pl.when(has_right)
    def _():
        signal(barrier, subj=subj + CORES)

    signal(barrier, subj=sibling)
    signal_perms(barrier)
    pl.semaphore_wait(
        barrier, n_perm + has_left.astype(jnp.int32) + has_right.astype(jnp.int32))

    def wave_right():
        @pl.when(has_left)
        def _():
            pl.semaphore_wait(waves.at[0], 1)

        @pl.when(has_right)
        def _():
            signal(waves.at[0], subj=subj + CORES)

    def wave_left():
        @pl.when(has_right)
        def _():
            pl.semaphore_wait(waves.at[1], 1)

        @pl.when(has_left)
        def _():
            signal(waves.at[1], subj=subj - CORES)

    def all_ready():
        @pl.when(z < n_z // 2)
        def _():
            wave_right()
            wave_left()

        @pl.when(z >= n_z // 2)
        def _():
            wave_left()
            wave_right()

        signal(waves.at[2], subj=sibling)
        pl.semaphore_wait(waves.at[2], 1)
        signal_perms(waves.at[3])
        pl.semaphore_wait(waves.at[3], n_perm - 1)

    def half(h):
        return pl.ds(pl.multiple_of(h * piece, piece), piece)

    def own_copy(h, way, target):
        return pltpu.make_async_remote_copy(
            src_ref=phe_ref.at[half(h), pl.ds(first_col, cols)],
            dst_ref=gathered.at[subj, half(h)],
            send_sem=own_send.at[way, h], recv_sem=row_recv.at[subj, h],
            device_id={"subj": target}, device_id_type=MESH)

    def pass_copy(slot, h, sems, target):
        return pltpu.make_async_remote_copy(
            src_ref=gathered.at[slot, half(h)], dst_ref=gathered.at[slot, half(h)],
            send_sem=sems.at[slot, h], recv_sem=row_recv.at[slot, h],
            device_id={"subj": target}, device_id_type=MESH)

    def shuf_copy(k, slot):
        return pltpu.make_async_remote_copy(
            src_ref=shf_ref, dst_ref=shuf.at[slot],
            send_sem=shuf_send.at[k], recv_sem=shuf_recv.at[slot],
            device_id=partner(k)[1], device_id_type=MESH)

    def own_sends(first, last, act):
        for h in range(first, last):
            @pl.when(z > 0)
            def _():
                act(own_copy(h, 0, subj - CORES))

            @pl.when(z < n_z - 1)
            def _():
                act(own_copy(h, 1, subj + CORES))

            act(own_copy(h, 2, sibling))

    own_sends(0, HALVES - 1, lambda copy: copy.start())
    all_ready()

    @pl.loop(1, n_all)
    def _(k):
        shuf_copy(k, me).start()

    own_sends(HALVES - 1, HALVES, lambda copy: copy.start())
    shuf[me] = shf_ref[...]
    for load in loads:
        load.wait()
    own32 = gathered[subj].astype(jnp.float32)
    squares = jnp.sum(own32 * own32, axis=0, keepdims=True)
    for p in range(n_perm):
        parts[p, 1:2] = squares
    own_cols = pl.ds(pl.multiple_of(subj * rows, rows), rows)
    down = lax.broadcasted_iota(jnp.int32, (rows, rows), 0)
    across = lax.broadcasted_iota(jnp.int32, (rows, rows), 1)
    kin_diag = jnp.sum(
        jnp.where(down == across, kin_ref[:, own_cols].astype(jnp.float32), 0.0),
        axis=1, keepdims=True)

    def move(task):
        p, block = task // n_subj, lax.rem(task, n_subj)
        base = down + block * rows
        picks = jnp.concatenate(
            [(base == shuf[p * n_subj + j]).astype(jnp.bfloat16) for j in range(n_subj)],
            axis=1)
        kin = lax.dot_general(
            kin_ref[...], picks, (((1,), (1,)), ((), ())),
            preferred_element_type=jnp.float32)
        at = pl.multiple_of(p * 2 * rows, 2 * rows)
        moved_kin[block, pl.ds(at, rows)] = kin.astype(jnp.bfloat16)
        picker = (scol[p] == across + block * rows).astype(jnp.bfloat16)
        moved_kin[block, pl.ds(at + rows, rows)] = picker

    def event(e, act):
        dist, h = e // HALVES + 1, lax.rem(e, HALVES)

        @pl.when(z + dist < n_z)
        def _():
            act(subj + CORES * dist, h, z > 0, subj - CORES)

        @pl.when(z - dist >= 0)
        def _():
            act(subj - CORES * dist, h, z < n_z - 1, subj + CORES)

    def arrive(slot, h, onward, target):
        pass_copy(slot, h, row_send, sibling).wait_recv()

        @pl.when(onward)
        def _():
            pass_copy(slot, h, row_send, target).start()

        pass_copy(slot, h, sib_send, sibling).start()

    def drain(slot, h, onward, target):
        @pl.when(onward)
        def _():
            pass_copy(slot, h, row_send, target).wait_send()

        pass_copy(slot, h, sib_send, sibling).wait_send()

    def add(slot):
        acc[...] += jnp.dot(
            moved_kin[slot], gathered[slot], preferred_element_type=jnp.float32)

    def await_sibling(slot):
        for h in range(HALVES):
            pass_copy(slot, h, row_send, sibling).wait_recv()

    def add_dist(dist):
        def pair(slot, other):
            add(slot)
            await_sibling(other)
            add(other)

        flip = sibling - subj

        @pl.when(z + dist < n_z)
        def _():
            pair(subj + CORES * dist, subj + CORES * dist + flip)

        @pl.when(jnp.logical_and(z - dist >= 0, dist > 0))
        def _():
            pair(subj - CORES * dist, subj - CORES * dist + flip)

    n_tasks = n_perm * n_subj
    busy = HALVES * n_z // 2
    per_event = n_tasks // busy
    early = min(BEFORE + busy, n_events)
    acc[...] = jnp.zeros_like(acc)
    for e in range(BEFORE):
        event(e, arrive)

    @pl.loop(1, n_all)
    def _(k):
        shuf_copy(k, partner(k)[0]).wait_recv()

    for p in range(n_perm):
        mine = shuf[p * n_subj + subj]
        scol[p] = jnp.transpose(jnp.broadcast_to(mine, (rows, rows)))

    @pl.loop(0, busy)
    def _(turn):
        @pl.loop(0, per_event)
        def _(t):
            move(turn * per_event + t)

        e = BEFORE + turn

        event(e, arrive)

    late = n_events - early

    @pl.loop(0, late)
    def _(turn):
        @pl.loop(turn * (n_z - 1) // late, (turn + 1) * (n_z - 1) // late)
        def _(dist):
            add_dist(dist)

        event(early + turn, arrive)

    add_dist(n_z - 1)

    for p in range(n_perm):
        at = p * 2 * rows
        moved = acc[at + rows:at + 2 * rows]
        cross = jnp.sum(moved * (acc[at:at + rows] - kin_diag * moved), axis=0, keepdims=True)
        parts[p, 0:1] = cross

    per_z = n_all // n_z
    far_low = (z >= n_z // 2).astype(jnp.int32)

    def fin_copy(k, slot):
        turn, rest = k // per_z, lax.rem(k, per_z)
        to_z = far_low * turn + (1 - far_low) * (n_z - 1 - turn)
        to_perm, to_subj = rest // CORES, to_z * CORES + lax.rem(rest, CORES)
        copy = pltpu.make_async_remote_copy(
            src_ref=parts.at[to_perm], dst_ref=final.at[slot],
            send_sem=fin_send.at[k], recv_sem=fin_recv.at[slot],
            device_id={"perm": to_perm, "subj": to_subj}, device_id_type=MESH)
        return copy, to_perm * n_subj + to_subj != me

    @pl.loop(0, n_all)
    def _(k):
        copy, other = fin_copy(k, me)
        pl.when(other)(copy.start)

    final[me] = parts[perm]
    own_sends(0, HALVES, lambda copy: copy.wait_send())

    @pl.loop(0, n_events)
    def _(e):
        event(e, drain)

    @pl.loop(1, n_all)
    def _(k):
        shuf_copy(k, me).wait_send()

    @pl.loop(1, n_all)
    def _(k):
        fin_copy(0, partner(k)[0])[0].wait_recv()

    count = n_subj * rows
    for q in range(n_perm):
        total = jnp.sum(final[q * n_subj:(q + 1) * n_subj], axis=0)
        scale = jnp.sqrt(jnp.float32(count)) * (total[1:2] / count + 1e-05)
        out_ref[:, q * cols:(q + 1) * cols] = total[0:1] / scale

    @pl.loop(0, n_all)
    def _(k):
        copy, other = fin_copy(k, me)
        pl.when(other)(copy.wait_send)


def per_device(n_perm, n_subj, kinship, phenotype, shuffle):
    rows, width = phenotype.shape
    cols = width // n_perm
    n_all = n_perm * n_subj
    DMA = pltpu.SemaphoreType.DMA
    out = pl.pallas_call(
        functools.partial(kernel, n_perm, n_subj),
        out_shape=jax.ShapeDtypeStruct((1, width), jnp.float32),
        in_specs=[pl.BlockSpec(memory_space=pl.ANY)] * 2 + [pl.BlockSpec(memory_space=pltpu.VMEM)],
        out_specs=pl.BlockSpec(memory_space=pltpu.VMEM),
        scratch_shapes=[
            pltpu.VMEM(kinship.shape, jnp.bfloat16),
            DMA((2,)),
            pltpu.SemaphoreType.REGULAR((4,)),
            pltpu.VMEM((n_all, 1, rows), jnp.int32),
            pltpu.VMEM((n_perm, rows, rows), jnp.int32),
            pltpu.VMEM((n_subj, n_perm * 2 * rows, rows), jnp.bfloat16),
            pltpu.VMEM((n_subj, rows, cols), jnp.bfloat16),
            pltpu.VMEM((n_perm * 2 * rows, cols), jnp.float32),
            pltpu.VMEM((n_perm, 2, cols), jnp.float32),
            pltpu.VMEM((n_all, 2, cols), jnp.float32),
            DMA((n_all,)), DMA((n_all,)),
            DMA((3, HALVES)),
            DMA((n_subj, HALVES)), DMA((n_subj, HALVES)), DMA((n_subj, HALVES)),
            DMA((n_all,)), DMA((n_all,)),
        ],
        compiler_params=pltpu.CompilerParams(collective_id=0, has_side_effects=True),
    )(kinship, phenotype, shuffle.reshape(1, rows))
    return out.reshape(width)


def solution(mesh):
    in_specs = (P("subj", None), P("subj", "vert"), P(("perm", "subj")))
    out_specs = P(("perm", "vert"))
    body = functools.partial(per_device, mesh.shape["perm"], mesh.shape["subj"])
    return jax.shard_map(body, mesh=mesh, in_specs=in_specs, out_specs=out_specs, check_vma=False)
```

profile of v0, /device:TPU:0, one launch (start us, length us, event | category | flops | bytes accessed | tf_op | source)
XLA Modules:
  0.0 33.8 jit_solution(391036056867472700)
XLA Ops:
  0.0 32.5 %shard_map.37 = f32[1,1024]{1,0:T(1,128)} custom-call(bf16[256,2048]{1,0:T(8,128)(2,1)} %kin_hbm.1, bf16[256,1024]{1,0:T(8,128)(2,1)} %phe_ref.1, s32[1,256]{1,0:T(1,128)} %bitcast.3), custom_call_target="tpu_custom_call" | custom-call | tf_op jit(solution)/shard_map/pallas_call | solution.py:318
  32.5 1.3 %copy.5 = f32[1024]{0:T(1024)} copy(f32[1024]{0:T(1024)} %bitcast.2) | data formatting | bytes 8192
where the time goes:
time: 34 us; the launch traced here: 33.8 us
  Pallas kernels  32.5 us (96%)
  local copies, waits for them, and re-layouts  1.28 us (4%)
    pallas_call x1, Pallas kernels, per_device(): pl.pallas_call(functools.partial(kernel, n_perm, n_subj), out_shape=jax.S...  32.5 us
    unnamed x1, local copies, waits for them, and re-layouts  1.28 us

commit v1 on v0

v1 whole, which is shorter than its diff:
```python
import functools

import jax
import jax.numpy as jnp
from jax import lax
from jax.experimental import pallas as pl
from jax.experimental.pallas import tpu as pltpu
from jax.sharding import PartitionSpec as P

MESH = pl.DeviceIdType.MESH
CORES = 2
PIECES = 4
SHARED = 3
SPAN = 4


def kernel(
    n_perm, n_subj, n_vert,
    kin_hbm, phe_hbm, shf_hbm, out_ref,
    kin, end_kin, kin_t, end_t, shuf, moved, gathered, acc, parts, final,
    load_sem, up, peers, lines,
    shuf_recv, shuf_own, shuf_in,
    row_recv, own_send, row_send, sib_send,
    end_recv, end_send, end_share, fin_send, fin_recv,
):
    perm, subj, vert = lax.axis_index("perm"), lax.axis_index("subj"), lax.axis_index("vert")
    n_all = n_perm * n_subj
    me = perm * n_subj + subj
    z, core = subj // CORES, lax.rem(subj, CORES)
    n_z = n_subj // CORES
    last = n_z - 1
    sibling = z * CORES + (1 - core)
    rows, cols = kin.shape[0], gathered.shape[2]
    piece = rows // PIECES
    n_list = kin.shape[1] // rows
    n_spans = gathered.shape[0] // SPAN
    n_plane = n_perm * CORES
    n_in = n_vert * n_plane
    n_chips = n_vert * n_perm
    chip = vert * n_perm + perm
    share = rows // n_chips
    place = chip * CORES + core
    inner = jnp.logical_and(z > 0, z < last)
    by_end = jnp.logical_or(z == 1, z == last - 1)
    first_col = pl.multiple_of(perm * cols, cols)
    barrier = pltpu.get_barrier_semaphore()

    def signal(sem, **device):
        pl.semaphore_signal(sem, inc=1, device_id=device, device_id_type=MESH)

    def in_plane(t):
        return dict(vert=t // n_plane, perm=lax.rem(t // CORES, n_perm), subj=z * CORES + lax.rem(t, CORES))

    def half(h):
        return pl.ds(pl.multiple_of(h * piece, piece), piece)

    def spot(q, c, h):
        at = pl.multiple_of(lax.rem(h, 2) * (2 * piece) + c * piece, piece)
        return gathered.at[q * 2 + h // 2, pl.ds(at, piece)]

    near = jnp.where(z * 2 < n_z, 0, last)
    far = last - near
    low_end = near == 0
    far_core = jnp.where(low_end, core, 1 - core)

    def listed(l):
        if l == 0:
            return near * CORES + core
        if l == 1:
            return near * CORES + 1 - core
        if l == 2:
            return far * CORES + far_core
        if l == 3:
            return far * CORES + 1 - far_core
        if l == 4:
            return subj
        if l == 5:
            return sibling
        k = l - 5
        other = jnp.where(k < z, k, k + 1)
        return other * CORES + jnp.where(other > z, core, 1 - core)

    def kin_load(l):
        block = pl.multiple_of(listed(l) * rows, rows)
        return pltpu.make_async_copy(
            kin_hbm.at[:, pl.ds(block, rows)], kin.at[:, l * rows:(l + 1) * rows], load_sem.at[PIECES + l])

    def phe_load(h):
        return pltpu.make_async_copy(
            phe_hbm.at[half(h), pl.ds(first_col, cols)], spot(z, core, h), load_sem.at[h])

    loads = [functools.partial(kin_load, l) for l in range(n_list)]
    loads += [functools.partial(phe_load, h) for h in range(PIECES)]

    @pl.loop(z + 1, n_z)
    def _(q):
        signal(barrier, subj=q * CORES + core)

    @pl.loop(place + 1, n_in)
    def _(t):
        signal(barrier, **in_plane(t))

    @pl.when(z + place > 0)
    def _():
        pl.semaphore_wait(barrier, z + place)

    @pl.loop(1, z + 1)
    def _(d):
        signal(up.at[d], subj=subj - CORES * d)

    @pl.loop(0, place)
    def _(t):
        signal(peers, **in_plane(t))

    def remote(src, dst, send, recv, **device):
        return pltpu.make_async_remote_copy(
            src_ref=src, dst_ref=dst, send_sem=send, recv_sem=recv, device_id=device, device_id_type=MESH)

    def own_copy(h, way, target):
        return remote(
            phe_hbm.at[half(h), pl.ds(first_col, cols)], spot(z, core, h),
            own_send.at[way, h], row_recv.at[subj, h], subj=target)

    def pass_copy(slot, h, sems, target):
        here = spot(slot // CORES, lax.rem(slot, CORES), h)
        return remote(here, here, sems.at[slot, h], row_recv.at[slot, h], subj=target)

    def shuf_own_copy(q):
        return remote(shf_hbm, shuf.at[me], shuf_own.at[q], shuf_recv.at[me], subj=q * CORES + core)

    def shuf_wait(slot):
        remote(shuf.at[slot], shuf.at[slot], shuf_own.at[0], shuf_recv.at[slot], subj=sibling).wait_recv()

    def shuf_in_copy(src, slot, k):
        t = lax.rem(perm * CORES + core + k, n_plane)
        line = slot - perm * n_subj
        return remote(src, shuf.at[slot], shuf_in.at[line, k], shuf_recv.at[slot],
                      perm=t // CORES, subj=z * CORES + lax.rem(t, CORES))

    def part_of(owner):
        return pl.ds(pl.multiple_of(owner * share, share), share)

    def end_block(i):
        end_core = core if i == 0 else 1 - core
        if i < 2:
            return z * CORES + end_core
        return jnp.where(z == 0, last * CORES + core, 1 - core)

    def end_copy(i, target):
        block = pl.multiple_of(end_block(i) * rows, rows)
        return remote(
            kin_hbm.at[part_of(chip), pl.ds(block, rows)], end_kin.at[part_of(chip), i * rows:(i + 1) * rows],
            end_send.at[i], end_recv.at[chip, i], subj=target)

    def end_share_copy(i, owner, t):
        here = end_kin.at[part_of(owner), i * rows:(i + 1) * rows]
        return remote(here, here, end_share.at[i, t], end_recv.at[owner, i], vert=t // n_perm, perm=lax.rem(t, n_perm))

    def send_ends(target, act):
        @pl.when(jnp.logical_not(inner))
        def _():
            for i in range(SHARED):
                act(end_copy(i, target))

    def send_rows(way, target, act):
        for h in range(PIECES):
            act(own_copy(h, way, target))

    def start(copy):
        copy.start()

    def finish(copy):
        copy.wait_send()

    to_low, to_high = z >= 2, z <= last - 2

    @pl.when(to_low)
    def _():
        @pl.loop(1, z)
        def _(k):
            shuf_own_copy(z - k).start()

        send_ends(subj - CORES, start)
        send_rows(0, subj - CORES, start)

    @pl.when(inner)
    def _():
        for load in loads:
            load().start()

    @pl.when(to_high)
    def _():
        pl.semaphore_wait(up.at[1], 1)
        shuf_own_copy(z + 1).start()
        send_ends(subj + CORES, start)

        @pl.loop(2, last - z)
        def _(d):
            pl.semaphore_wait(up.at[d], 1)
            shuf_own_copy(z + d).start()

        send_rows(1, subj + CORES, start)

    @pl.when(place < n_in - 1)
    def _():
        pl.semaphore_wait(peers, n_in - 1 - place)

    def event(dist, h, act):
        @pl.when(z + dist < n_z)
        def _():
            act(subj + CORES * dist, h, z > 1, subj - CORES)

        @pl.when(z - dist >= 0)
        def _():
            act(subj - CORES * dist, h, z < last - 1, subj + CORES)

    def arrive(slot, h, onward, target):
        pass_copy(slot, h, row_send, sibling).wait_recv()

        @pl.when(onward)
        def _():
            pass_copy(slot, h, row_send, target).start()

        pass_copy(slot, h, sib_send, sibling).start()

    def drain(slot, h, onward, target):
        @pl.when(onward)
        def _():
            pass_copy(slot, h, row_send, target).wait_send()

        pass_copy(slot, h, sib_send, sibling).wait_send()

    def shuf_arrive(subj_slot, h, onward, target):
        slot = perm * n_subj + subj_slot
        shuf_wait(slot)
        for k in range(1, n_plane):
            shuf_in_copy(shuf.at[slot], slot, k).start()

    def shuf_drain(subj_slot, h, onward, target):
        slot = perm * n_subj + subj_slot
        for k in range(1, n_plane):
            shuf_in_copy(shuf.at[slot], slot, k).wait_send()

    span = SPAN * rows
    spot_row = lax.broadcasted_iota(jnp.int32, (span, rows), 0)
    spot_id = (
        spot_row // (2 * piece) * piece // rows * (CORES * rows) + lax.rem(spot_row // (2 * piece) * piece, rows)
        + lax.rem(spot_row // piece, 2) * rows + lax.rem(spot_row, piece))

    def picks_of(p, turn, l):
        ids = spot_id + turn * span
        return (ids == shuf[p * n_subj + listed(l)]).astype(jnp.bfloat16)

    def move_own(task):
        p, turn = task // n_spans, lax.rem(task, n_spans)
        picks = [picks_of(p, turn, l) for l in range(n_list)]
        out = jnp.dot(jnp.concatenate(picks, axis=1), kin_t[...], preferred_element_type=jnp.float32)
        at = pl.ds(pl.multiple_of(turn * span, span), span)
        moved[2 * p, at] = out.astype(jnp.bfloat16)
        moved[2 * p + 1, at] = picks[4]
        moved[2 * (n_perm + p) + 1, at] = picks[0]

    def move_end(task):
        p, turn = task // n_spans, lax.rem(task, n_spans)
        picks = [picks_of(p, turn, l) for l in range(SHARED)]
        out = jnp.dot(jnp.concatenate(picks, axis=1), end_t[...], preferred_element_type=jnp.float32)
        at = pl.ds(pl.multiple_of(turn * span, span), span)
        moved[2 * (n_perm + p), at] = out.astype(jnp.bfloat16)

    n_half = n_perm * 2

    def add(chunks, part, first=False):
        for q in range(part * n_half, (part + 1) * n_half):
            total = None if first else acc[q]
            for chunk in chunks:
                at = pl.ds(pl.multiple_of(chunk * rows, rows), rows)
                term = lax.dot_general(
                    moved[q, at], gathered[chunk], (((0,), (0,)), ((), ())), preferred_element_type=jnp.float32)
                total = term if total is None else total + term
            acc[q] = total

    def sides(dist, act):
        @pl.loop(0, 2)
        def _(side):
            q = z + dist * (1 - 2 * side)

            @pl.when(jnp.logical_and(q >= 0, q < n_z))
            def _():
                act(q)

    def await_sibling(q, hs):
        for h in hs:
            pass_copy(q * CORES + 1 - core, h, row_send, sibling).wait_recv()

    def turn_block(src, dst, l, scale, clear=False):
        block = jnp.transpose(src[:, l * rows:(l + 1) * rows].astype(jnp.float32)) * scale
        if clear:
            down = lax.broadcasted_iota(jnp.int32, (rows, rows), 0)
            across = lax.broadcasted_iota(jnp.int32, (rows, rows), 1)
            block = jnp.where(down == across, 0.0, block)
        dst[l * rows:(l + 1) * rows] = block.astype(jnp.bfloat16)

    def square_sum(chunk):
        own = gathered[chunk].astype(jnp.float32)
        return jnp.sum(own * own, axis=0, keepdims=True)

    n_tasks = n_perm * n_spans
    turns = PIECES

    per_hub = n_subj - 2 * CORES

    def hub_slot(p, s):
        return p * per_hub + s - CORES

    per_z = n_all // n_z

    def fin_copy(k):
        to_z, rest = k // per_z, lax.rem(k, per_z)
        to_perm, to_subj = rest // CORES, to_z * CORES + lax.rem(rest, CORES)
        mine = hub_slot(perm, subj)
        copy = remote(parts.at[to_perm], final.at[mine], fin_send.at[k], fin_recv.at[mine],
                      perm=to_perm, subj=to_subj)
        return copy, to_perm * n_subj + to_subj != me

    @pl.when(inner)
    def _():
        for k in range(1, n_plane):
            shuf_in_copy(shf_hbm, me, k).start()
        for h in range(PIECES):
            own_copy(h, 2, sibling).start()
        own_shuf = pltpu.make_async_copy(shf_hbm, shuf.at[me], load_sem.at[PIECES + n_list])
        own_shuf.start()
        own_shuf.wait()
        for load in loads:
            load().wait()
        for l in range(n_list):
            turn_block(kin, kin_t, l, 0.5 if l in (4, 5) else 1.0, clear=l == 4)

        @pl.loop(1, last)
        def _(dist):
            event(dist, 0, shuf_arrive)

        @pl.when(by_end)
        def _():
            for i in range(SHARED):
                end_share_copy(i, chip, chip).wait_recv()
                for k in range(1, n_chips):
                    end_share_copy(i, chip, lax.rem(chip + k, n_chips)).start()

        @pl.loop(jnp.where(to_high, last - z, 1), n_z - z)
        def _(d):
            pl.semaphore_wait(up.at[d], 1)

        for k in range(1, n_plane):
            t = lax.rem(perm * CORES + core + k, n_plane)
            signal(lines, perm=t // CORES, subj=z * CORES + lax.rem(t, CORES))

        @pl.loop(1, n_plane)
        def _(k):
            t = lax.rem(perm * CORES + core + k, n_plane)

            @pl.loop(0, n_z)
            def _(q):
                slot = (t // CORES) * n_subj + q * CORES + lax.rem(t, CORES)
                shuf_wait(slot)

        @pl.loop(0, turns)
        def _(turn):
            event(1, turn, arrive)

            @pl.loop(turn * n_tasks // turns, (turn + 1) * n_tasks // turns)
            def _(task):
                move_own(task)

        await_sibling(z, range(PIECES))
        parts[0, 1:2] = square_sum(z * 2 + core)
        add([z * 2, z * 2 + 1], 0, first=True)
        event(2, 0, arrive)

        def add_own(q):
            await_sibling(q, range(PIECES))
            add([q * 2, q * 2 + 1], 0)

        sides(1, add_own)
        event(2, 1, arrive)

        @pl.when(by_end)
        def _():
            @pl.loop(1, n_chips)
            def _(k):
                for i in range(SHARED):
                    end_share_copy(i, lax.rem(chip + k, n_chips), chip).wait_recv()

            for l in range(SHARED):
                turn_block(end_kin, end_t, l, 0.5 if l < 2 else 1.0, clear=l == 0)
            parts[0, 1:2] += square_sum(near * 2 + core)

        @pl.when(jnp.logical_not(by_end))
        def _():
            end_t[...] = jnp.zeros_like(end_t)

        for p in range(1, n_perm):
            parts[p, 1:2] = parts[0, 1:2]

        @pl.loop(0, 2)
        def _(turn):
            @pl.loop(turn * n_tasks // 2, (turn + 1) * n_tasks // 2)
            def _(task):
                move_end(task)

            event(2, 2 + turn, arrive)

        add([z * 2, z * 2 + 1], 1, first=True)
        sides(1, lambda q: add([q * 2, q * 2 + 1], 1))

        def add_all(q):
            for j in range(2):
                await_sibling(q, range(2 * j, 2 * j + 2))
                for part in range(2):
                    add([q * 2 + j], part)

        sides(2, add_all)
        if last > 3:
            @pl.loop(3, last)
            def _(dist):
                for h in range(PIECES):
                    event(dist, h, arrive)
                sides(dist, add_all)

        for p in range(n_perm):
            cross = 0.0
            for part in range(2):
                at = (part * n_perm + p) * 2
                cross += jnp.sum(acc[at] * acc[at + 1], axis=0, keepdims=True)
            parts[p, 0:1] = cross

        pl.semaphore_wait(lines, n_plane - 1)

        @pl.loop(0, n_all)
        def _(k):
            copy, other = fin_copy(k)
            pl.when(other)(copy.start)

        final[hub_slot(perm, subj)] = parts[perm]

    @pl.loop(0, n_perm)
    def _(p):
        @pl.loop(CORES, n_subj - CORES)
        def _(s):
            @pl.when(p * n_subj + s != me)
            def _():
                slot = hub_slot(p, s)
                remote(parts.at[0], final.at[slot], fin_send.at[0], fin_recv.at[slot], subj=sibling).wait_recv()

    count = n_subj * rows
    for q in range(n_perm):
        total = jnp.sum(final[q * per_hub:(q + 1) * per_hub], axis=0)
        scale = jnp.sqrt(jnp.float32(count)) * (total[1:2] / count + 1e-05)
        out_ref[:, q * cols:(q + 1) * cols] = 2.0 * total[0:1] / scale

    @pl.when(to_low)
    def _():
        @pl.loop(1, z)
        def _(k):
            shuf_own_copy(z - k).wait_send()

        send_ends(subj - CORES, finish)
        send_rows(0, subj - CORES, finish)

    @pl.when(to_high)
    def _():
        @pl.loop(1, last - z)
        def _(d):
            shuf_own_copy(z + d).wait_send()

        send_ends(subj + CORES, finish)
        send_rows(1, subj + CORES, finish)

    @pl.when(z == 0)
    def _():
        pl.semaphore_wait(up.at[last], 1)

    @pl.when(inner)
    def _():
        for k in range(1, n_plane):
            shuf_in_copy(shf_hbm, me, k).wait_send()
        for h in range(PIECES):
            own_copy(h, 2, sibling).wait_send()

        @pl.loop(1, last)
        def _(dist):
            event(dist, 0, shuf_drain)
            for h in range(PIECES):
                event(dist, h, drain)

        @pl.when(by_end)
        def _():
            for i in range(SHARED):
                for k in range(1, n_chips):
                    end_share_copy(i, chip, lax.rem(chip + k, n_chips)).wait_send()

        @pl.loop(0, n_all)
        def _(k):
            copy, other = fin_copy(k)
            pl.when(other)(copy.wait_send)


def per_device(n_perm, n_subj, n_vert, kinship, phenotype, shuffle):
    rows, width = phenotype.shape
    cols = width // n_perm
    n_all = n_perm * n_subj
    n_z = n_subj // CORES
    n_list = n_z + 3
    n_chips = n_vert * n_perm
    n_hubs = n_perm * (n_subj - 2 * CORES)
    DMA, VMEM = pltpu.SemaphoreType.DMA, pltpu.VMEM
    out = pl.pallas_call(
        functools.partial(kernel, n_perm, n_subj, n_vert),
        out_shape=jax.ShapeDtypeStruct((1, width), jnp.float32),
        in_specs=[pl.BlockSpec(memory_space=pl.ANY)] * 3,
        out_specs=pl.BlockSpec(memory_space=VMEM),
        scratch_shapes=[
            VMEM((rows, n_list * rows), jnp.bfloat16),
            VMEM((rows, SHARED * rows), jnp.bfloat16),
            VMEM((n_list * rows, rows), jnp.bfloat16),
            VMEM((SHARED * rows, rows), jnp.bfloat16),
            VMEM((n_all, 1, rows), jnp.int32),
            VMEM((n_perm * 4, n_subj * rows, rows), jnp.bfloat16),
            VMEM((n_z * 2, rows, cols), jnp.bfloat16),
            VMEM((n_perm * 4, rows, cols), jnp.float32),
            VMEM((n_perm, 2, cols), jnp.float32),
            VMEM((n_hubs, 2, cols), jnp.float32),
            DMA((PIECES + n_list + 1,)),
            pltpu.SemaphoreType.REGULAR((n_z,)), pltpu.SemaphoreType.REGULAR, pltpu.SemaphoreType.REGULAR,
            DMA((n_all,)), DMA((n_z,)), DMA((n_subj, n_perm * CORES)),
            DMA((n_subj, PIECES)), DMA((3, PIECES)), DMA((n_subj, PIECES)), DMA((n_subj, PIECES)),
            DMA((n_chips, SHARED)), DMA((SHARED,)), DMA((SHARED, n_chips)),
            DMA((n_all,)), DMA((n_hubs,)),
        ],
        compiler_params=pltpu.CompilerParams(collective_id=0, has_side_effects=True),
    )(kinship, phenotype, shuffle.reshape(1, rows))
    return out.reshape(width)


def solution(mesh):
    in_specs = (P("subj", None), P("subj", "vert"), P(("perm", "subj")))
    out_specs = P(("perm", "vert"))
    sizes = [mesh.shape[axis] for axis in ("perm", "subj", "vert")]
    body = functools.partial(per_device, *sizes)
    return jax.shard_map(body, mesh=mesh, in_specs=in_specs, out_specs=out_specs, check_vma=False)
```

time: 34 us -> 33 us (0.971)
  Pallas kernels: 32.5 us -> 31.5 us
    pallas_call x1, Pallas kernels: 32.5 us -> 31.5 us  [per_device(): pl.pallas_call(functools.partial(kernel, n_perm, n_subj, n_vert), out_sha...]
where the time goes in v1:
time: 33 us; the launch traced here: 32.8 us
  Pallas kernels  31.5 us (95%)
  local copies, waits for them, and re-layouts  1.28 us (4%)
    pallas_call x1, Pallas kernels, per_device(): pl.pallas_call(functools.partial(kernel, n_perm, n_subj, n_vert), out_sha...  31.5 us
    unnamed x1, local copies, waits for them, and re-layouts  1.28 us

profile of v1, /device:TPU:0, one launch (start us, length us, event | category | flops | bytes accessed | tf_op | source)
XLA Modules:
  0.0 32.8 jit_solution(10771152004096755645)
XLA Ops:
  0.0 31.5 %shard_map.37 = f32[1,1024]{1,0:T(1,128)} custom-call(bf16[256,2048]{1,0:T(8,128)(2,1)} %kin_hbm.1, bf16[256,1024]{1,0:T(8,128)(2,1)} %phe_hbm.1, s32[1,256]{1,0:T(1,128)} %bitcast.3), custom_call_target="tpu_custom_call" | custom-call | tf_op jit(solution)/shard_map/pallas_call | solution.py:517
  31.5 1.3 %copy.5 = f32[1024]{0:T(1024)} copy(f32[1024]{0:T(1024)} %bitcast.2) | data formatting | bytes 8192

commit v2 on v1

--- a/solution.py
+++ b/solution.py
@@ -12,13 +12,14 @@
 PIECES = 4
 SHARED = 3
 SPAN = 4
+END_SPAN = 4
 
 
 def kernel(
     n_perm, n_subj, n_vert,
     kin_hbm, phe_hbm, shf_hbm, out_ref,
     kin, end_kin, kin_t, end_t, shuf, moved, gathered, acc, parts, final,
-    load_sem, up, peers, lines,
+    load_sem, up, side, across_perm, across_vert, lines,
     shuf_recv, shuf_own, shuf_in,
     row_recv, own_send, row_send, sib_send,
     end_recv, end_send, end_share, fin_send, fin_recv,
@@ -30,16 +31,14 @@
     n_z = n_subj // CORES
     last = n_z - 1
     sibling = z * CORES + (1 - core)
-    rows, cols = kin.shape[0], gathered.shape[2]
+    rows, cols = kin.shape[0], gathered.shape[1]
     piece = rows // PIECES
     n_list = kin.shape[1] // rows
-    n_spans = gathered.shape[0] // SPAN
+    n_spans = gathered.shape[0] // (SPAN * rows)
     n_plane = n_perm * CORES
-    n_in = n_vert * n_plane
     n_chips = n_vert * n_perm
     chip = vert * n_perm + perm
     share = rows // n_chips
-    place = chip * CORES + core
     inner = jnp.logical_and(z > 0, z < last)
     by_end = jnp.logical_or(z == 1, z == last - 1)
     first_col = pl.multiple_of(perm * cols, cols)
@@ -48,15 +47,12 @@
     def signal(sem, **device):
         pl.semaphore_signal(sem, inc=1, device_id=device, device_id_type=MESH)
 
-    def in_plane(t):
-        return dict(vert=t // n_plane, perm=lax.rem(t // CORES, n_perm), subj=z * CORES + lax.rem(t, CORES))
-
     def half(h):
         return pl.ds(pl.multiple_of(h * piece, piece), piece)
 
     def spot(q, c, h):
-        at = pl.multiple_of(lax.rem(h, 2) * (2 * piece) + c * piece, piece)
-        return gathered.at[q * 2 + h // 2, pl.ds(at, piece)]
+        at = pl.multiple_of((q * PIECES + h) * (CORES * piece) + c * piece, piece)
+        return gathered.at[pl.ds(at, piece)]
 
     near = jnp.where(z * 2 < n_z, 0, last)
     far = last - near
@@ -89,6 +85,7 @@
         return pltpu.make_async_copy(
             phe_hbm.at[half(h), pl.ds(first_col, cols)], spot(z, core, h), load_sem.at[h])
 
+    own_shuf = pltpu.make_async_copy(shf_hbm, shuf.at[me], load_sem.at[PIECES + n_list])
     loads = [functools.partial(kin_load, l) for l in range(n_list)]
     loads += [functools.partial(phe_load, h) for h in range(PIECES)]
 
@@ -96,21 +93,58 @@
     def _(q):
         signal(barrier, subj=q * CORES + core)
 
-    @pl.loop(place + 1, n_in)
-    def _(t):
-        signal(barrier, **in_plane(t))
-
-    @pl.when(z + place > 0)
-    def _():
-        pl.semaphore_wait(barrier, z + place)
+    axes = (
+        (perm, n_perm, lambda d: dict(perm=perm + d)),
+        (vert, n_vert, lambda d: dict(vert=vert + d)),
+        (core, CORES, lambda d: dict(subj=subj + d)),
+    )
+    for index, size, near_by in axes:
+        @pl.when(jnp.logical_and(inner, index < size - 1))
+        def _():
+            signal(barrier, **near_by(1))
+
+    lower = sum((index > 0).astype(jnp.int32) for index, _, _ in axes)
+    lower = z + jnp.where(inner, lower, 0)
+
+    @pl.when(lower > 0)
+    def _():
+        pl.semaphore_wait(barrier, lower)
 
     @pl.loop(1, z + 1)
     def _(d):
         signal(up.at[d], subj=subj - CORES * d)
 
-    @pl.loop(0, place)
-    def _(t):
-        signal(peers, **in_plane(t))
+    def answer_plane():
+        for i, (index, size, near_by) in enumerate(axes):
+            @pl.when(index > 0)
+            def _():
+                signal(side.at[i], **near_by(-1))
+
+    def meet(i):
+        index, size, _ = axes[i]
+
+        @pl.when(index < size - 1)
+        def _():
+            pl.semaphore_wait(side.at[i], 1)
+
+    def sweep_ways(sem, i):
+        index, size, near_by = axes[i]
+        up_side, down_side = index < size - 1, index > 0
+        return (
+            (sem.at[0], lambda done: signal(done, **near_by(1)), down_side, up_side),
+            (sem.at[1], lambda done: signal(done, **near_by(-1)), up_side, down_side),
+        )
+
+    def launch(sem, i):
+        for done, tell, behind, ahead in sweep_ways(sem, i):
+            pl.when(jnp.logical_and(ahead, jnp.logical_not(behind)))(functools.partial(tell, done))
+
+    def finish_sweep(sem, i):
+        for done, tell, behind, ahead in sweep_ways(sem, i):
+            @pl.when(behind)
+            def _():
+                pl.semaphore_wait(done, 1)
+                pl.when(ahead)(functools.partial(tell, done))
 
     def remote(src, dst, send, recv, **device):
         return pltpu.make_async_remote_copy(
@@ -174,6 +208,8 @@
 
     to_low, to_high = z >= 2, z <= last - 2
 
+    pl.when(inner)(answer_plane)
+
     @pl.when(to_low)
     def _():
         @pl.loop(1, z)
@@ -187,6 +223,7 @@
     def _():
         for load in loads:
             load().start()
+        own_shuf.start()
 
     @pl.when(to_high)
     def _():
@@ -200,10 +237,6 @@
             shuf_own_copy(z + d).start()
 
         send_rows(1, subj + CORES, start)
-
-    @pl.when(place < n_in - 1)
-    def _():
-        pl.semaphore_wait(peers, n_in - 1 - place)
 
     def event(dist, h, act):
         @pl.when(z + dist < n_z)
@@ -241,43 +274,44 @@
         for k in range(1, n_plane):
             shuf_in_copy(shuf.at[slot], slot, k).wait_send()
 
-    span = SPAN * rows
-    spot_row = lax.broadcasted_iota(jnp.int32, (span, rows), 0)
-    spot_id = (
-        spot_row // (2 * piece) * piece // rows * (CORES * rows) + lax.rem(spot_row // (2 * piece) * piece, rows)
-        + lax.rem(spot_row // piece, 2) * rows + lax.rem(spot_row, piece))
-
-    def picks_of(p, turn, l):
-        ids = spot_id + turn * span
-        return (ids == shuf[p * n_subj + listed(l)]).astype(jnp.bfloat16)
+    in_piece = lax.broadcasted_iota(jnp.int32, (piece, rows), 0)
+
+    def picks_of(p, first, span, l):
+        line = shuf[p * n_subj + listed(l)] - first
+        bases = [
+            g // (PIECES * CORES) * (CORES * rows) + g // CORES % PIECES * piece + g % CORES * rows
+            for g in range(span // piece)]
+        return jnp.concatenate([(in_piece == line - base).astype(jnp.bfloat16) for base in bases], axis=0)
+
+    span, end_span = SPAN * rows, END_SPAN * rows
+    n_ends = gathered.shape[0] // end_span
 
     def move_own(task):
         p, turn = task // n_spans, lax.rem(task, n_spans)
-        picks = [picks_of(p, turn, l) for l in range(n_list)]
+        picks = [picks_of(p, turn * span, span, l) for l in range(n_list)]
         out = jnp.dot(jnp.concatenate(picks, axis=1), kin_t[...], preferred_element_type=jnp.float32)
         at = pl.ds(pl.multiple_of(turn * span, span), span)
         moved[2 * p, at] = out.astype(jnp.bfloat16)
         moved[2 * p + 1, at] = picks[4]
         moved[2 * (n_perm + p) + 1, at] = picks[0]
 
-    def move_end(task):
-        p, turn = task // n_spans, lax.rem(task, n_spans)
-        picks = [picks_of(p, turn, l) for l in range(SHARED)]
+    def move_end(p, turn):
+        picks = [picks_of(p, turn * end_span, end_span, l) for l in range(SHARED)]
         out = jnp.dot(jnp.concatenate(picks, axis=1), end_t[...], preferred_element_type=jnp.float32)
-        at = pl.ds(pl.multiple_of(turn * span, span), span)
+        at = pl.ds(pl.multiple_of(turn * end_span, end_span), end_span)
         moved[2 * (n_perm + p), at] = out.astype(jnp.bfloat16)
 
     n_half = n_perm * 2
 
-    def add(chunks, part, first=False):
-        for q in range(part * n_half, (part + 1) * n_half):
-            total = None if first else acc[q]
-            for chunk in chunks:
-                at = pl.ds(pl.multiple_of(chunk * rows, rows), rows)
-                term = lax.dot_general(
-                    moved[q, at], gathered[chunk], (((0,), (0,)), ((), ())), preferred_element_type=jnp.float32)
-                total = term if total is None else total + term
-            acc[q] = total
+    def term(q, start, length):
+        at = pl.ds(pl.multiple_of(start, rows), length)
+        return lax.dot_general(
+            moved[q, at], gathered[at], (((0,), (0,)), ((), ())), preferred_element_type=jnp.float32)
+
+    def add(which, start, length, first=False):
+        for q in which:
+            new = term(q, start, length)
+            acc[q] = new if first else acc[q] + new
 
     def sides(dist, act):
         @pl.loop(0, 2)
@@ -301,11 +335,9 @@
         dst[l * rows:(l + 1) * rows] = block.astype(jnp.bfloat16)
 
     def square_sum(chunk):
-        own = gathered[chunk].astype(jnp.float32)
+        own = gathered[pl.ds(pl.multiple_of(chunk * rows, rows), rows)].astype(jnp.float32)
         return jnp.sum(own * own, axis=0, keepdims=True)
 
-    n_tasks = n_perm * n_spans
-    turns = PIECES
 
     per_hub = n_subj - 2 * CORES
 
@@ -324,114 +356,170 @@
 
     @pl.when(inner)
     def _():
-        for k in range(1, n_plane):
-            shuf_in_copy(shf_hbm, me, k).start()
+        meet(2)
         for h in range(PIECES):
             own_copy(h, 2, sibling).start()
-        own_shuf = pltpu.make_async_copy(shf_hbm, shuf.at[me], load_sem.at[PIECES + n_list])
-        own_shuf.start()
-        own_shuf.wait()
+        meet(0)
+        launch(across_perm, 0)
+        meet(1)
         for load in loads:
             load().wait()
         for l in range(n_list):
             turn_block(kin, kin_t, l, 0.5 if l in (4, 5) else 1.0, clear=l == 4)
 
-        @pl.loop(1, last)
-        def _(dist):
-            event(dist, 0, shuf_arrive)
-
-        @pl.when(by_end)
-        def _():
-            for i in range(SHARED):
+        finish_sweep(across_perm, 0)
+        launch(across_vert, 1)
+        for k in range(1, n_plane):
+            shuf_in_copy(shf_hbm, me, k).start()
+
+        def share_end(i):
+            @pl.when(by_end)
+            def _():
                 end_share_copy(i, chip, chip).wait_recv()
                 for k in range(1, n_chips):
                     end_share_copy(i, chip, lax.rem(chip + k, n_chips)).start()
 
-        @pl.loop(jnp.where(to_high, last - z, 1), n_z - z)
-        def _(d):
-            pl.semaphore_wait(up.at[d], 1)
-
-        for k in range(1, n_plane):
-            t = lax.rem(perm * CORES + core + k, n_plane)
-            signal(lines, perm=t // CORES, subj=z * CORES + lax.rem(t, CORES))
-
-        @pl.loop(1, n_plane)
-        def _(k):
-            t = lax.rem(perm * CORES + core + k, n_plane)
-
-            @pl.loop(0, n_z)
-            def _(q):
-                slot = (t // CORES) * n_subj + q * CORES + lax.rem(t, CORES)
-                shuf_wait(slot)
-
-        @pl.loop(0, turns)
-        def _(turn):
-            event(1, turn, arrive)
-
-            @pl.loop(turn * n_tasks // turns, (turn + 1) * n_tasks // turns)
+        def meet_lines():
+            @pl.loop(jnp.where(to_high, last - z, 1), n_z - z)
+            def _(d):
+                pl.semaphore_wait(up.at[d], 1)
+
+            for k in range(1, n_plane):
+                t = lax.rem(perm * CORES + core + k, n_plane)
+                signal(lines, perm=t // CORES, subj=z * CORES + lax.rem(t, CORES))
+
+        def await_shuf(p):
+            for c in range(CORES):
+                @pl.when(p * CORES + c != perm * CORES + core)
+                def _():
+                    @pl.loop(0, n_z)
+                    def _(q):
+                        shuf_wait(p * n_subj + q * CORES + c)
+
+        def own_tasks(p, first, end):
+            @pl.loop(p * n_spans + first, p * n_spans + end)
             def _(task):
                 move_own(task)
 
-        await_sibling(z, range(PIECES))
-        parts[0, 1:2] = square_sum(z * 2 + core)
-        add([z * 2, z * 2 + 1], 0, first=True)
-        event(2, 0, arrive)
-
-        def add_own(q):
-            await_sibling(q, range(PIECES))
-            add([q * 2, q * 2 + 1], 0)
-
-        sides(1, add_own)
-        event(2, 1, arrive)
-
-        @pl.when(by_end)
-        def _():
-            @pl.loop(1, n_chips)
-            def _(k):
-                for i in range(SHARED):
-                    end_share_copy(i, lax.rem(chip + k, n_chips), chip).wait_recv()
-
-            for l in range(SHARED):
-                turn_block(end_kin, end_t, l, 0.5 if l < 2 else 1.0, clear=l == 0)
-            parts[0, 1:2] += square_sum(near * 2 + core)
-
-        @pl.when(jnp.logical_not(by_end))
-        def _():
-            end_t[...] = jnp.zeros_like(end_t)
-
-        for p in range(1, n_perm):
-            parts[p, 1:2] = parts[0, 1:2]
-
-        @pl.loop(0, 2)
-        def _(turn):
-            @pl.loop(turn * n_tasks // 2, (turn + 1) * n_tasks // 2)
-            def _(task):
-                move_end(task)
-
-            event(2, 2 + turn, arrive)
-
-        add([z * 2, z * 2 + 1], 1, first=True)
-        sides(1, lambda q: add([q * 2, q * 2 + 1], 1))
-
-        def add_all(q):
-            for j in range(2):
-                await_sibling(q, range(2 * j, 2 * j + 2))
-                for part in range(2):
-                    add([q * 2 + j], part)
-
-        sides(2, add_all)
-        if last > 3:
-            @pl.loop(3, last)
+        def end_tasks(p):
+            @pl.loop(0, n_ends)
+            def _(turn):
+                move_end(p, turn)
+
+        def take_ends():
+            @pl.when(by_end)
+            def _():
+                @pl.loop(1, n_chips)
+                def _(k):
+                    for i in range(SHARED):
+                        end_share_copy(i, lax.rem(chip + k, n_chips), chip).wait_recv()
+
+                for l in range(SHARED):
+                    turn_block(end_kin, end_t, l, 0.5 if l < 2 else 1.0, clear=l == 0)
+
+            @pl.when(jnp.logical_not(by_end))
+            def _():
+                end_t[...] = jnp.zeros_like(end_t)
+
+        def square_parts():
+            parts[0, 1:2] = square_sum(z * 2 + core)
+
+            @pl.when(by_end)
+            def _():
+                parts[0, 1:2] += square_sum(near * 2 + core)
+
+            for p in range(1, n_perm):
+                parts[p, 1:2] = parts[0, 1:2]
+
+        other_hub = last - z
+
+        def hub_piece(h):
+            arrive(other_hub * CORES + core, h, z < 0, subj)
+
+        def near_piece(h):
+            arrive(near * CORES + core, h, z > 0, other_hub * CORES + core)
+
+        def far_piece(h):
+            arrive(far * CORES + core, h, z < 0, subj)
+
+        plane_rows = CORES * rows
+        own_m, own_p = [2 * p for p in range(n_perm)], [2 * p + 1 for p in range(n_perm)]
+        end_m, end_p = ([n_half + q for q in part] for part in (own_m, own_p))
+        short = last == 3
+
+        turns = [lax.rem(perm + k, n_perm) for k in range(n_perm)]
+        event(1, 0, shuf_arrive)
+        finish_sweep(across_vert, 1)
+        share_end(0)
+
+        @pl.loop(2, last)
+        def _(dist):
+            event(dist, 0, shuf_arrive)
+
+        own_shuf.wait()
+        share_end(1)
+        share_end(2)
+        await_shuf(turns[0])
+        if short:
+            own_tasks(turns[0], 0, n_spans // 2)
+            near_piece(0)
+            hub_piece(0)
+            hub_piece(1)
+            own_tasks(turns[0], n_spans // 2, n_spans)
+            near_piece(1)
+            hub_piece(2)
+            for turn in turns[1:]:
+                await_shuf(turn)
+                own_tasks(turn, 0, n_spans // 2)
+                near_piece(2)
+                hub_piece(3)
+                own_tasks(turn, n_spans // 2, n_spans)
+            near_piece(3)
+            meet_lines()
+            take_ends()
+            for p in range(n_perm):
+                end_tasks(p)
+                far_piece(p)
+            for q in (z, other_hub, near):
+                await_sibling(q, range(PIECES))
+            square_parts()
+            start = (z - 1) * plane_rows
+            add(own_m + own_p, start, 3 * plane_rows, first=True)
+            far_piece(2)
+            add(end_p, start, 3 * plane_rows, first=True)
+            far_piece(3)
+            add(end_m, start, 3 * plane_rows, first=True)
+        else:
+            for k, turn in enumerate(turns):
+                if k > 0:
+                    await_shuf(turn)
+                own_tasks(turn, 0, n_spans)
+
+            @pl.loop(1, last)
             def _(dist):
                 for h in range(PIECES):
                     event(dist, h, arrive)
-                sides(dist, add_all)
-
+
+            meet_lines()
+            await_sibling(z, range(PIECES))
+            for dist in range(1, last):
+                sides(dist, lambda q: await_sibling(q, range(PIECES)))
+            add(own_m + own_p + end_p, plane_rows, (n_z - 2) * plane_rows, first=True)
+            take_ends()
+            for p in range(n_perm):
+                end_tasks(p)
+            square_parts()
+            add(end_m, plane_rows, (n_z - 2) * plane_rows, first=True)
+            add(own_m + own_p + end_p + end_m, near * plane_rows, plane_rows)
+        if short:
+            await_sibling(far, range(PIECES))
+        start = far * plane_rows
         for p in range(n_perm):
             cross = 0.0
             for part in range(2):
-                at = (part * n_perm + p) * 2
-                cross += jnp.sum(acc[at] * acc[at + 1], axis=0, keepdims=True)
+                q = part * n_half + 2 * p
+                left, right = (acc[i] + term(i, start, plane_rows) for i in (q, q + 1))
+                cross += jnp.sum(left * right, axis=0, keepdims=True)
             parts[p, 0:1] = cross
 
         pl.semaphore_wait(lines, n_plane - 1)
@@ -526,12 +614,13 @@
             VMEM((SHARED * rows, rows), jnp.bfloat16),
             VMEM((n_all, 1, rows), jnp.int32),
             VMEM((n_perm * 4, n_subj * rows, rows), jnp.bfloat16),
-            VMEM((n_z * 2, rows, cols), jnp.bfloat16),
+            VMEM((n_subj * rows, cols), jnp.bfloat16),
             VMEM((n_perm * 4, rows, cols), jnp.float32),
             VMEM((n_perm, 2, cols), jnp.float32),
             VMEM((n_hubs, 2, cols), jnp.float32),
             DMA((PIECES + n_list + 1,)),
-            pltpu.SemaphoreType.REGULAR((n_z,)), pltpu.SemaphoreType.REGULAR, pltpu.SemaphoreType.REGULAR,
+            pltpu.SemaphoreType.REGULAR((n_z,)), pltpu.SemaphoreType.REGULAR((3,)),
+            pltpu.SemaphoreType.REGULAR((2,)), pltpu.SemaphoreType.REGULAR((2,)), pltpu.SemaphoreType.REGULAR,
             DMA((n_all,)), DMA((n_z,)), DMA((n_subj, n_perm * CORES)),
             DMA((n_subj, PIECES)), DMA((3, PIECES)), DMA((n_subj, PIECES)), DMA((n_subj, PIECES)),
             DMA((n_chips, SHARED)), DMA((SHARED,)), DMA((SHARED, n_chips)),

time: 33 us -> 31.1 us (0.942)
  Pallas kernels: 31.5 us -> 29.6 us
    pallas_call x1, Pallas kernels: 31.5 us -> 29.6 us  [per_device(): pl.pallas_call(functools.partial(kernel, n_perm, n_subj, n_vert), out_sha...]
where the time goes in v2:
time: 31.1 us; the launch traced here: 30.9 us
  Pallas kernels  29.6 us (95%)
  local copies, waits for them, and re-layouts  1.28 us (4%)
    pallas_call x1, Pallas kernels, per_device(): pl.pallas_call(functools.partial(kernel, n_perm, n_subj, n_vert), out_sha...  29.6 us
    unnamed x1, local copies, waits for them, and re-layouts  1.28 us

profile of v2, /device:TPU:0, one launch (start us, length us, event | category | flops | bytes accessed | tf_op | source)
XLA Modules:
  0.0 30.9 jit_solution(15702357265013691657)
XLA Ops:
  0.0 29.6 %shard_map.37 = f32[1,1024]{1,0:T(1,128)} custom-call(bf16[256,2048]{1,0:T(8,128)(2,1)} %kin_hbm.1, bf16[256,1024]{1,0:T(8,128)(2,1)} %phe_hbm.1, s32[1,256]{1,0:T(1,128)} %bitcast.3), custom_call_target="tpu_custom_call" | custom-call | tf_op jit(solution)/shard_map/pallas_call | solution.py:605
  29.7 1.3 %copy.5 = f32[1024]{0:T(1024)} copy(f32[1024]{0:T(1024)} %bitcast.2) | data formatting | bytes 8192

commit v3 on v2

--- a/solution.py
+++ b/solution.py
@@ -18,11 +18,11 @@
 def kernel(
     n_perm, n_subj, n_vert,
     kin_hbm, phe_hbm, shf_hbm, out_ref,
-    kin, end_kin, kin_t, end_t, shuf, moved, gathered, acc, parts, final,
+    kin, end_kin, kin_t, end_t, shuf, moved, gathered, acc, parts, final, sent,
     load_sem, up, side, across_perm, across_vert, lines,
-    shuf_recv, shuf_own, shuf_in,
-    row_recv, own_send, row_send, sib_send,
-    end_recv, end_send, end_share, fin_send, fin_recv,
+    line_recv, group_recv, shuf_own, shuf_in,
+    row_recv, sib_recv, own_send, row_send, sib_send,
+    end_recv, peer_recv, end_send, end_share, fin_send, fin_recv,
 ):
     perm, subj, vert = lax.axis_index("perm"), lax.axis_index("subj"), lax.axis_index("vert")
     n_all = n_perm * n_subj
@@ -79,13 +79,13 @@
     def kin_load(l):
         block = pl.multiple_of(listed(l) * rows, rows)
         return pltpu.make_async_copy(
-            kin_hbm.at[:, pl.ds(block, rows)], kin.at[:, l * rows:(l + 1) * rows], load_sem.at[PIECES + l])
+            kin_hbm.at[:, pl.ds(block, rows)], kin.at[:, l * rows:(l + 1) * rows], load_sem.at[0])
 
     def phe_load(h):
         return pltpu.make_async_copy(
-            phe_hbm.at[half(h), pl.ds(first_col, cols)], spot(z, core, h), load_sem.at[h])
-
-    own_shuf = pltpu.make_async_copy(shf_hbm, shuf.at[me], load_sem.at[PIECES + n_list])
+            phe_hbm.at[half(h), pl.ds(first_col, cols)], spot(z, core, h), load_sem.at[1])
+
+    own_shuf = pltpu.make_async_copy(shf_hbm, shuf.at[me], load_sem.at[2])
     loads = [functools.partial(kin_load, l) for l in range(n_list)]
     loads += [functools.partial(phe_load, h) for h in range(PIECES)]
 
@@ -150,25 +150,36 @@
         return pltpu.make_async_remote_copy(
             src_ref=src, dst_ref=dst, send_sem=send, recv_sem=recv, device_id=device, device_id_type=MESH)
 
+    def await_sent(ref, sem):
+        remote(ref, ref, sem, sem, subj=sibling).wait_send()
+
+    def await_all(ref, sem):
+        remote(ref, ref, sem, sem, subj=sibling).wait_recv()
+
     def own_copy(h, way, target):
         return remote(
             phe_hbm.at[half(h), pl.ds(first_col, cols)], spot(z, core, h),
-            own_send.at[way, h], row_recv.at[subj, h], subj=target)
-
-    def pass_copy(slot, h, sems, target):
-        here = spot(slot // CORES, lax.rem(slot, CORES), h)
-        return remote(here, here, sems.at[slot, h], row_recv.at[slot, h], subj=target)
+            own_send.at[way], row_recv.at[z, h], subj=target)
+
+    def own_sib_copy(h):
+        return remote(
+            phe_hbm.at[half(h), pl.ds(first_col, cols)], spot(z, core, h), sib_send, sib_recv.at[z], subj=sibling)
+
+    def pass_copy(q, h, target):
+        here = spot(q, core, h)
+        return remote(here, here, row_send.at[q], row_recv.at[q, h], subj=target)
+
+    def sib_copy(q, h):
+        here = spot(q, core, h)
+        return remote(here, here, sib_send, sib_recv.at[q], subj=sibling)
 
     def shuf_own_copy(q):
-        return remote(shf_hbm, shuf.at[me], shuf_own.at[q], shuf_recv.at[me], subj=q * CORES + core)
-
-    def shuf_wait(slot):
-        remote(shuf.at[slot], shuf.at[slot], shuf_own.at[0], shuf_recv.at[slot], subj=sibling).wait_recv()
-
-    def shuf_in_copy(src, slot, k):
+        return remote(shf_hbm, shuf.at[me], shuf_own, line_recv.at[z], subj=q * CORES + core)
+
+    def shuf_in_copy(src, q, k):
         t = lax.rem(perm * CORES + core + k, n_plane)
-        line = slot - perm * n_subj
-        return remote(src, shuf.at[slot], shuf_in.at[line, k], shuf_recv.at[slot],
+        slot = perm * n_subj + q * CORES + core
+        return remote(src, shuf.at[slot], shuf_in, group_recv.at[perm * CORES + core],
                       perm=t // CORES, subj=z * CORES + lax.rem(t, CORES))
 
     def part_of(owner):
@@ -184,27 +195,21 @@
         block = pl.multiple_of(end_block(i) * rows, rows)
         return remote(
             kin_hbm.at[part_of(chip), pl.ds(block, rows)], end_kin.at[part_of(chip), i * rows:(i + 1) * rows],
-            end_send.at[i], end_recv.at[chip, i], subj=target)
+            end_send, end_recv.at[i], subj=target)
 
     def end_share_copy(i, owner, t):
         here = end_kin.at[part_of(owner), i * rows:(i + 1) * rows]
-        return remote(here, here, end_share.at[i, t], end_recv.at[owner, i], vert=t // n_perm, perm=lax.rem(t, n_perm))
-
-    def send_ends(target, act):
+        return remote(here, here, end_share, peer_recv, vert=t // n_perm, perm=lax.rem(t, n_perm))
+
+    def send_ends(target):
         @pl.when(jnp.logical_not(inner))
         def _():
             for i in range(SHARED):
-                act(end_copy(i, target))
-
-    def send_rows(way, target, act):
+                end_copy(i, target).start()
+
+    def send_rows(way, target):
         for h in range(PIECES):
-            act(own_copy(h, way, target))
-
-    def start(copy):
-        copy.start()
-
-    def finish(copy):
-        copy.wait_send()
+            own_copy(h, way, target).start()
 
     to_low, to_high = z >= 2, z <= last - 2
 
@@ -216,8 +221,8 @@
         def _(k):
             shuf_own_copy(z - k).start()
 
-        send_ends(subj - CORES, start)
-        send_rows(0, subj - CORES, start)
+        send_ends(subj - CORES)
+        send_rows(0, subj - CORES)
 
     @pl.when(inner)
     def _():
@@ -229,50 +234,43 @@
     def _():
         pl.semaphore_wait(up.at[1], 1)
         shuf_own_copy(z + 1).start()
-        send_ends(subj + CORES, start)
+        send_ends(subj + CORES)
 
         @pl.loop(2, last - z)
         def _(d):
             pl.semaphore_wait(up.at[d], 1)
             shuf_own_copy(z + d).start()
 
-        send_rows(1, subj + CORES, start)
+        send_rows(1, subj + CORES)
 
     def event(dist, h, act):
         @pl.when(z + dist < n_z)
         def _():
-            act(subj + CORES * dist, h, z > 1, subj - CORES)
+            act(z + dist, h, z > 1, subj - CORES)
 
         @pl.when(z - dist >= 0)
         def _():
-            act(subj - CORES * dist, h, z < last - 1, subj + CORES)
-
-    def arrive(slot, h, onward, target):
-        pass_copy(slot, h, row_send, sibling).wait_recv()
+            act(z - dist, h, z < last - 1, subj + CORES)
+
+    def arrive(q, h, onward, target):
+        pass_copy(q, h, sibling).wait_recv()
 
         @pl.when(onward)
         def _():
-            pass_copy(slot, h, row_send, target).start()
-
-        pass_copy(slot, h, sib_send, sibling).start()
-
-    def drain(slot, h, onward, target):
+            pass_copy(q, h, target).start()
+
+        sib_copy(q, h).start()
+
+    def drain(q, h, onward, target):
         @pl.when(onward)
         def _():
-            pass_copy(slot, h, row_send, target).wait_send()
-
-        pass_copy(slot, h, sib_send, sibling).wait_send()
-
-    def shuf_arrive(subj_slot, h, onward, target):
-        slot = perm * n_subj + subj_slot
-        shuf_wait(slot)
+            await_sent(gathered.at[0:rows], row_send.at[q])
+
+    def shuf_arrive(q, h, onward, target):
+        slot = perm * n_subj + q * CORES + core
+        await_all(shuf.at[slot], line_recv.at[q])
         for k in range(1, n_plane):
-            shuf_in_copy(shuf.at[slot], slot, k).start()
-
-    def shuf_drain(subj_slot, h, onward, target):
-        slot = perm * n_subj + subj_slot
-        for k in range(1, n_plane):
-            shuf_in_copy(shuf.at[slot], slot, k).wait_send()
+            shuf_in_copy(shuf.at[slot], q, k).start()
 
     in_piece = lax.broadcasted_iota(jnp.int32, (piece, rows), 0)
 
@@ -322,9 +320,8 @@
             def _():
                 act(q)
 
-    def await_sibling(q, hs):
-        for h in hs:
-            pass_copy(q * CORES + 1 - core, h, row_send, sibling).wait_recv()
+    def await_sibling(q):
+        await_all(gathered.at[0:rows], sib_recv.at[q])
 
     def turn_block(src, dst, l, scale, clear=False):
         block = jnp.transpose(src[:, l * rows:(l + 1) * rows].astype(jnp.float32)) * scale
@@ -350,7 +347,7 @@
         to_z, rest = k // per_z, lax.rem(k, per_z)
         to_perm, to_subj = rest // CORES, to_z * CORES + lax.rem(rest, CORES)
         mine = hub_slot(perm, subj)
-        copy = remote(parts.at[to_perm], final.at[mine], fin_send.at[k], fin_recv.at[mine],
+        copy = remote(parts.at[to_perm], final.at[mine], fin_send, fin_recv,
                       perm=to_perm, subj=to_subj)
         return copy, to_perm * n_subj + to_subj != me
 
@@ -358,24 +355,24 @@
     def _():
         meet(2)
         for h in range(PIECES):
-            own_copy(h, 2, sibling).start()
+            own_sib_copy(h).start()
         meet(0)
         launch(across_perm, 0)
         meet(1)
-        for load in loads:
-            load().wait()
+        pltpu.make_async_copy(kin, kin, load_sem.at[0]).wait()
+        pltpu.make_async_copy(gathered.at[0:rows], gathered.at[0:rows], load_sem.at[1]).wait()
         for l in range(n_list):
             turn_block(kin, kin_t, l, 0.5 if l in (4, 5) else 1.0, clear=l == 4)
 
         finish_sweep(across_perm, 0)
         launch(across_vert, 1)
         for k in range(1, n_plane):
-            shuf_in_copy(shf_hbm, me, k).start()
+            shuf_in_copy(shf_hbm, z, k).start()
 
         def share_end(i):
             @pl.when(by_end)
             def _():
-                end_share_copy(i, chip, chip).wait_recv()
+                end_copy(i, sibling).wait_recv()
                 for k in range(1, n_chips):
                     end_share_copy(i, chip, lax.rem(chip + k, n_chips)).start()
 
@@ -392,9 +389,7 @@
             for c in range(CORES):
                 @pl.when(p * CORES + c != perm * CORES + core)
                 def _():
-                    @pl.loop(0, n_z)
-                    def _(q):
-                        shuf_wait(p * n_subj + q * CORES + c)
+                    await_all(shuf.at[0:n_z], group_recv.at[p * CORES + c])
 
         def own_tasks(p, first, end):
             @pl.loop(p * n_spans + first, p * n_spans + end)
@@ -409,11 +404,7 @@
         def take_ends():
             @pl.when(by_end)
             def _():
-                @pl.loop(1, n_chips)
-                def _(k):
-                    for i in range(SHARED):
-                        end_share_copy(i, lax.rem(chip + k, n_chips), chip).wait_recv()
-
+                await_all(end_kin.at[0:(n_chips - 1) * share], peer_recv)
                 for l in range(SHARED):
                     turn_block(end_kin, end_t, l, 0.5 if l < 2 else 1.0, clear=l == 0)
 
@@ -434,13 +425,13 @@
         other_hub = last - z
 
         def hub_piece(h):
-            arrive(other_hub * CORES + core, h, z < 0, subj)
+            arrive(other_hub, h, z < 0, subj)
 
         def near_piece(h):
-            arrive(near * CORES + core, h, z > 0, other_hub * CORES + core)
+            arrive(near, h, z > 0, other_hub * CORES + core)
 
         def far_piece(h):
-            arrive(far * CORES + core, h, z < 0, subj)
+            arrive(far, h, z < 0, subj)
 
         plane_rows = CORES * rows
         own_m, own_p = [2 * p for p in range(n_perm)], [2 * p + 1 for p in range(n_perm)]
@@ -481,7 +472,7 @@
                 end_tasks(p)
                 far_piece(p)
             for q in (z, other_hub, near):
-                await_sibling(q, range(PIECES))
+                await_sibling(q)
             square_parts()
             start = (z - 1) * plane_rows
             add(own_m + own_p, start, 3 * plane_rows, first=True)
@@ -501,9 +492,9 @@
                     event(dist, h, arrive)
 
             meet_lines()
-            await_sibling(z, range(PIECES))
+            await_sibling(z)
             for dist in range(1, last):
-                sides(dist, lambda q: await_sibling(q, range(PIECES)))
+                sides(dist, lambda q: await_sibling(q))
             add(own_m + own_p + end_p, plane_rows, (n_z - 2) * plane_rows, first=True)
             take_ends()
             for p in range(n_perm):
@@ -512,7 +503,7 @@
             add(end_m, plane_rows, (n_z - 2) * plane_rows, first=True)
             add(own_m + own_p + end_p + end_m, near * plane_rows, plane_rows)
         if short:
-            await_sibling(far, range(PIECES))
+            await_sibling(far)
         start = far * plane_rows
         for p in range(n_perm):
             cross = 0.0
@@ -531,14 +522,15 @@
 
         final[hub_slot(perm, subj)] = parts[perm]
 
-    @pl.loop(0, n_perm)
-    def _(p):
-        @pl.loop(CORES, n_subj - CORES)
-        def _(s):
-            @pl.when(p * n_subj + s != me)
-            def _():
-                slot = hub_slot(p, s)
-                remote(parts.at[0], final.at[slot], fin_send.at[0], fin_recv.at[slot], subj=sibling).wait_recv()
+    n_hubs = n_perm * per_hub
+
+    @pl.when(inner)
+    def _():
+        await_all(final.at[0:n_hubs - 1], fin_recv)
+
+    @pl.when(jnp.logical_not(inner))
+    def _():
+        await_all(final, fin_recv)
 
     count = n_subj * rows
     for q in range(n_perm):
@@ -546,51 +538,35 @@
         scale = jnp.sqrt(jnp.float32(count)) * (total[1:2] / count + 1e-05)
         out_ref[:, q * cols:(q + 1) * cols] = 2.0 * total[0:1] / scale
 
-    @pl.when(to_low)
-    def _():
-        @pl.loop(1, z)
-        def _(k):
-            shuf_own_copy(z - k).wait_send()
-
-        send_ends(subj - CORES, finish)
-        send_rows(0, subj - CORES, finish)
-
-    @pl.when(to_high)
-    def _():
-        @pl.loop(1, last - z)
-        def _(d):
-            shuf_own_copy(z + d).wait_send()
-
-        send_ends(subj + CORES, finish)
-        send_rows(1, subj + CORES, finish)
-
-    @pl.when(z == 0)
-    def _():
-        pl.semaphore_wait(up.at[last], 1)
+    for way, sending in enumerate((to_low, to_high)):
+        @pl.when(sending)
+        def _():
+            await_sent(gathered.at[0:rows], own_send.at[way])
 
     @pl.when(inner)
     def _():
-        for k in range(1, n_plane):
-            shuf_in_copy(shf_hbm, me, k).wait_send()
-        for h in range(PIECES):
-            own_copy(h, 2, sibling).wait_send()
+        await_sent(shuf.at[0:n_z - 3], shuf_own)
+        await_sent(shuf.at[0:n_z * (n_plane - 1)], shuf_in)
+        await_sent(gathered.at[0:n_z * rows], sib_send)
 
         @pl.loop(1, last)
         def _(dist):
-            event(dist, 0, shuf_drain)
-            for h in range(PIECES):
-                event(dist, h, drain)
+            event(dist, 0, drain)
 
         @pl.when(by_end)
         def _():
-            for i in range(SHARED):
-                for k in range(1, n_chips):
-                    end_share_copy(i, chip, lax.rem(chip + k, n_chips)).wait_send()
-
-        @pl.loop(0, n_all)
-        def _(k):
-            copy, other = fin_copy(k)
-            pl.when(other)(copy.wait_send)
+            await_sent(end_kin.at[0:(n_chips - 1) * share], end_share)
+
+        await_sent(sent, fin_send)
+
+    @pl.when(jnp.logical_not(inner))
+    def _():
+        await_sent(shuf.at[0:n_z - 2], shuf_own)
+        await_sent(end_kin.at[0:share], end_send)
+
+    @pl.when(z == 0)
+    def _():
+        pl.semaphore_wait(up.at[last], 1)
 
 
 def per_device(n_perm, n_subj, n_vert, kinship, phenotype, shuffle):
@@ -618,13 +594,13 @@
             VMEM((n_perm * 4, rows, cols), jnp.float32),
             VMEM((n_perm, 2, cols), jnp.float32),
             VMEM((n_hubs, 2, cols), jnp.float32),
-            DMA((PIECES + n_list + 1,)),
+            VMEM((n_all - 1, 2, cols), jnp.float32),
+            DMA((3,)),
             pltpu.SemaphoreType.REGULAR((n_z,)), pltpu.SemaphoreType.REGULAR((3,)),
             pltpu.SemaphoreType.REGULAR((2,)), pltpu.SemaphoreType.REGULAR((2,)), pltpu.SemaphoreType.REGULAR,
-            DMA((n_all,)), DMA((n_z,)), DMA((n_subj, n_perm * CORES)),
-            DMA((n_subj, PIECES)), DMA((3, PIECES)), DMA((n_subj, PIECES)), DMA((n_subj, PIECES)),
-            DMA((n_chips, SHARED)), DMA((SHARED,)), DMA((SHARED, n_chips)),
-            DMA((n_all,)), DMA((n_hubs,)),
+            DMA((n_z,)), DMA((n_perm * CORES,)), DMA, DMA,
+            DMA((n_z, PIECES)), DMA((n_z,)), DMA((2,)), DMA((n_z,)), DMA,
+            DMA((SHARED,)), DMA, DMA, DMA, DMA, DMA,
         ],
         compiler_params=pltpu.CompilerParams(collective_id=0, has_side_effects=True),
     )(kinship, phenotype, shuffle.reshape(1, rows))

time: 31.1 us -> 29.4 us (0.945)
  Pallas kernels: 29.6 us -> 27.9 us
    pallas_call x1, Pallas kernels: 29.6 us -> 27.9 us  [per_device(): pl.pallas_call(functools.partial(kernel, n_perm, n_subj, n_vert), out_sha...]
where the time goes in v3:
time: 29.4 us; the launch traced here: 29.2 us
  Pallas kernels  27.9 us (95%)
  local copies, waits for them, and re-layouts  1.28 us (4%)
    pallas_call x1, Pallas kernels, per_device(): pl.pallas_call(functools.partial(kernel, n_perm, n_subj, n_vert), out_sha...  27.9 us
    unnamed x1, local copies, waits for them, and re-layouts  1.28 us

profile of v3, /device:TPU:0, one launch (start us, length us, event | category | flops | bytes accessed | tf_op | source)
XLA Modules:
  0.0 29.2 jit_solution(8022283595407092708)
XLA Ops:
  0.0 27.9 %shard_map.37 = f32[1,1024]{1,0:T(1,128)} custom-call(bf16[256,2048]{1,0:T(8,128)(2,1)} %kin_hbm.1, bf16[256,1024]{1,0:T(8,128)(2,1)} %phe_hbm.1, s32[1,256]{1,0:T(1,128)} %bitcast.3), custom_call_target="tpu_custom_call" | custom-call | tf_op jit(solution)/shard_map/pallas_call | solution.py:581
  27.9 1.3 %copy.5 = f32[1024]{0:T(1024)} copy(f32[1024]{0:T(1024)} %bitcast.2) | data formatting | bytes 8192

commit v4 on v3

--- a/solution.py
+++ b/solution.py
@@ -51,7 +51,7 @@
         return pl.ds(pl.multiple_of(h * piece, piece), piece)
 
     def spot(q, c, h):
-        at = pl.multiple_of((q * PIECES + h) * (CORES * piece) + c * piece, piece)
+        at = pl.multiple_of((q * CORES + c) * rows + h * piece, piece)
         return gathered.at[pl.ds(at, piece)]
 
     near = jnp.where(z * 2 < n_z, 0, last)
@@ -272,14 +272,9 @@
         for k in range(1, n_plane):
             shuf_in_copy(shuf.at[slot], q, k).start()
 
-    in_piece = lax.broadcasted_iota(jnp.int32, (piece, rows), 0)
-
     def picks_of(p, first, span, l):
-        line = shuf[p * n_subj + listed(l)] - first
-        bases = [
-            g // (PIECES * CORES) * (CORES * rows) + g // CORES % PIECES * piece + g % CORES * rows
-            for g in range(span // piece)]
-        return jnp.concatenate([(in_piece == line - base).astype(jnp.bfloat16) for base in bases], axis=0)
+        subject = lax.broadcasted_iota(jnp.int32, (span, rows), 0) + first
+        return (subject == shuf[p * n_subj + listed(l)]).astype(jnp.bfloat16)
 
     span, end_span = SPAN * rows, END_SPAN * rows
     n_ends = gathered.shape[0] // end_span
@@ -466,20 +461,20 @@
                 hub_piece(3)
                 own_tasks(turn, n_spans // 2, n_spans)
             near_piece(3)
+            far_piece(0)
             meet_lines()
             take_ends()
             for p in range(n_perm):
                 end_tasks(p)
-                far_piece(p)
+                far_piece(p + 1)
             for q in (z, other_hub, near):
                 await_sibling(q)
             square_parts()
             start = (z - 1) * plane_rows
             add(own_m + own_p, start, 3 * plane_rows, first=True)
-            far_piece(2)
-            add(end_p, start, 3 * plane_rows, first=True)
-            far_piece(3)
-            add(end_m, start, 3 * plane_rows, first=True)
+            for h in range(n_perm + 1, PIECES):
+                far_piece(h)
+            add(end_p + end_m, start, 3 * plane_rows, first=True)
         else:
             for k, turn in enumerate(turns):
                 if k > 0:

time: 29.4 us -> 28.3 us (0.963)
  Pallas kernels: 27.9 us -> 26.8 us
    pallas_call x1, Pallas kernels: 27.9 us -> 26.8 us  [per_device(): pl.pallas_call(functools.partial(kernel, n_perm, n_subj, n_vert), out_sha...]
where the time goes in v4:
time: 28.3 us; the launch traced here: 28.1 us
  Pallas kernels  26.8 us (95%)
  local copies, waits for them, and re-layouts  1.28 us (5%)
    pallas_call x1, Pallas kernels, per_device(): pl.pallas_call(functools.partial(kernel, n_perm, n_subj, n_vert), out_sha...  26.8 us
    unnamed x1, local copies, waits for them, and re-layouts  1.28 us

profile of v4, /device:TPU:0, one launch (start us, length us, event | category | flops | bytes accessed | tf_op | source)
XLA Modules:
  0.0 28.1 jit_solution(12582481748051530718)
XLA Ops:
  0.0 26.8 %shard_map.37 = f32[1,1024]{1,0:T(1,128)} custom-call(bf16[256,2048]{1,0:T(8,128)(2,1)} %kin_hbm.1, bf16[256,1024]{1,0:T(8,128)(2,1)} %phe_hbm.1, s32[1,256]{1,0:T(1,128)} %bitcast.3), custom_call_target="tpu_custom_call" | custom-call | tf_op jit(solution)/shard_map/pallas_call | solution.py:576
  26.8 1.3 %copy.5 = f32[1024]{0:T(1024)} copy(f32[1024]{0:T(1024)} %bitcast.2) | data formatting | bytes 8192

commit v5 on v4

--- a/solution.py
+++ b/solution.py
@@ -336,15 +336,13 @@
     def hub_slot(p, s):
         return p * per_hub + s - CORES
 
-    per_z = n_all // n_z
-
-    def fin_copy(k):
-        to_z, rest = k // per_z, lax.rem(k, per_z)
-        to_perm, to_subj = rest // CORES, to_z * CORES + lax.rem(rest, CORES)
-        mine = hub_slot(perm, subj)
-        copy = remote(parts.at[to_perm], final.at[mine], fin_send, fin_recv,
-                      perm=to_perm, subj=to_subj)
-        return copy, to_perm * n_subj + to_subj != me
+    def send_parts(p):
+        @pl.loop(0, n_subj)
+        def _(s):
+            @pl.when(p * n_subj + s != me)
+            def _():
+                mine = final.at[hub_slot(perm, subj)]
+                remote(parts.at[p], mine, fin_send, fin_recv, perm=p, subj=s).start()
 
     @pl.when(inner)
     def _():
@@ -499,6 +497,7 @@
             add(own_m + own_p + end_p + end_m, near * plane_rows, plane_rows)
         if short:
             await_sibling(far)
+        pl.semaphore_wait(lines, n_plane - 1)
         start = far * plane_rows
         for p in range(n_perm):
             cross = 0.0
@@ -507,13 +506,7 @@
                 left, right = (acc[i] + term(i, start, plane_rows) for i in (q, q + 1))
                 cross += jnp.sum(left * right, axis=0, keepdims=True)
             parts[p, 0:1] = cross
-
-        pl.semaphore_wait(lines, n_plane - 1)
-
-        @pl.loop(0, n_all)
-        def _(k):
-            copy, other = fin_copy(k)
-            pl.when(other)(copy.start)
+            send_parts(p)
 
         final[hub_slot(perm, subj)] = parts[perm]
 

time: 28.3 us -> 27.8 us (0.982)
  Pallas kernels: 26.8 us -> 26.4 us
    pallas_call x1, Pallas kernels: 26.8 us -> 26.4 us  [per_device(): pl.pallas_call(functools.partial(kernel, n_perm, n_subj, n_vert), out_sha...]
where the time goes in v5:
time: 27.8 us; the launch traced here: 27.6 us
  Pallas kernels  26.4 us (95%)
  local copies, waits for them, and re-layouts  1.28 us (5%)
    pallas_call x1, Pallas kernels, per_device(): pl.pallas_call(functools.partial(kernel, n_perm, n_subj, n_vert), out_sha...  26.4 us
    unnamed x1, local copies, waits for them, and re-layouts  1.28 us

profile of v5, /device:TPU:0, one launch (start us, length us, event | category | flops | bytes accessed | tf_op | source)
XLA Modules:
  0.0 27.6 jit_solution(7351865732273753113)
XLA Ops:
  0.0 26.4 %shard_map.37 = f32[1,1024]{1,0:T(1,128)} custom-call(bf16[256,2048]{1,0:T(8,128)(2,1)} %kin_hbm.1, bf16[256,1024]{1,0:T(8,128)(2,1)} %phe_hbm.1, s32[1,256]{1,0:T(1,128)} %bitcast.3), custom_call_target="tpu_custom_call" | custom-call | tf_op jit(solution)/shard_map/pallas_call | solution.py:569
  26.4 1.3 %copy.5 = f32[1024]{0:T(1024)} copy(f32[1024]{0:T(1024)} %bitcast.2) | data formatting | bytes 8192
